TPU v7x, 32 devices: a whole 2x2x4 slice. The times are simulated.
32 devices in a mesh: sec: 2 (over x), lat: 16 (over z, y, core).
Axes of the slice: x: 2, y: 2, z: 4, core: 2. Of those that a mesh axis runs over, the one named last changes fastest.
Arguments:
- resid_in: bfloat16 [4, 128, 2048], P('sec', None, 'lat'), may hold values from -6 to 6
- mlp_out: bfloat16 [4, 128, 2048], P('sec', None, 'lat'), may hold values from -6 to 6
- enc_weight: bfloat16 [4, 2048, 1024], P('sec', None, 'lat'), may hold values from -0.125 to 0.125
- enc_bias: float32 [4, 1024], P('sec', 'lat'), may hold values from -3 to 3
- thresholds: int32 [4, 1024], P('sec', 'lat'), may hold values from 0 to 3
- same_dec: bfloat16 [4, 1024, 2048], P('sec', 'lat'), may hold values from -0.1875 to 0.1875
- next_dec: bfloat16 [2, 1024, 2048], P('sec', 'lat'), may hold values from -0.1875 to 0.1875
- cross_dec: bfloat16 [2, 2, 1024, 2048], P('sec', None, 'lat'), may hold values from -0.1875 to 0.1875
Outputs:
- mean_square: float32 [], replicated
- grad_enc: bfloat16 [4, 2048, 1024], P('sec', None, 'lat')
- grad_bias: float32 [4, 1024], P('sec', 'lat')
- grad_same: bfloat16 [4, 1024, 2048], P('sec', 'lat')
- grad_next: bfloat16 [2, 1024, 2048], P('sec', 'lat')
- grad_cross: bfloat16 [2, 2, 1024, 2048], P('sec', None, 'lat')
All inputs are finite; a program needn't handle non-finite values.
Results may differ from a plain program's by a relative error of at most 0.0059.
Values may be sent and summed in bfloat16 or wider, within the bound.
No kernel may reach another device: no remote copies, remote signals or barrier semaphores. Data moves between devices by JAX's collectives and lax.ppermute only.
A program may use at most 64 MiB of HBM per device.

v0:
```python
import jax
import jax.numpy as jnp
from jax import lax
from jax.sharding import PartitionSpec as P

D = 2048
TOKENS = 128
jump_width = 0.1


def shifted(value, axis, steps):
    count = lax.axis_size(axis)
    first, last = (max(0, -steps), min(count, count - steps))
    return lax.ppermute(value, axis, [(source, source + steps) for source in range(first, last)])


def back_dot(grad, weights):
    return lax.dot_general(
        grad, weights, (((1,), (1,)), ((), ())), preferred_element_type=jnp.float32
    )


def outer_dot(act, grad):
    return lax.dot_general(act, grad, (((0,), (0,)), ((), ())), preferred_element_type=jnp.float32)


def per_device(resid_in, mlp_out, enc_weight, enc_bias, thresholds, same_dec, next_dec, cross_dec):
    leading = lax.axis_index("sec") == 0
    inputs_full = lax.all_gather(resid_in, "lat", axis=2, tiled=True)
    pre_act = (
        jnp.einsum("ktd,kdc->ktc", inputs_full, enc_weight, preferred_element_type=jnp.float32)
        + enc_bias[:, None, :]
    )
    cut_level = 0.25 * thresholds.astype(jnp.float32)[:, None, :]
    gate_value = jax.nn.sigmoid((pre_act - cut_level) / jump_width)
    latent_act = (pre_act * gate_value).astype(jnp.bfloat16)
    rebuilt_first = jnp.dot(latent_act[0], same_dec[0], preferred_element_type=jnp.float32)
    rebuilt_second = jnp.dot(
        latent_act[1], same_dec[1], preferred_element_type=jnp.float32
    ) + jnp.dot(latent_act[0], next_dec[0], preferred_element_type=jnp.float32)
    far_weight = shifted(cross_dec, "sec", -1)
    source_act = jnp.where(leading, latent_act, jnp.zeros_like(latent_act))
    near_part = jnp.einsum(
        "ktc,kcd->td", source_act, cross_dec[0], preferred_element_type=jnp.float32
    )
    far_part = jnp.einsum(
        "ktc,kcd->td", source_act, far_weight[0], preferred_element_type=jnp.float32
    )
    partials = jnp.stack([rebuilt_first, rebuilt_second, near_part, far_part])
    summed = lax.psum_scatter(partials, "lat", scatter_dimension=2, tiled=True)
    crossing = shifted(summed[2:], "sec", 1)
    rebuilt = summed[:2] + crossing
    misfit = rebuilt - mlp_out.astype(jnp.float32)
    squared_total = lax.psum(jnp.sum(misfit * misfit), ("sec", "lat"))
    mean_square = squared_total / (4.0 * TOKENS * D)
    dy_rows = misfit.astype(jnp.bfloat16)
    extra_rows = shifted(dy_rows, "sec", -1)
    grad_full = lax.all_gather(
        jnp.concatenate([dy_rows, extra_rows], axis=0), "lat", axis=2, tiled=True
    )
    act_grad = jnp.stack(
        [
            back_dot(grad_full[0], same_dec[0]) + back_dot(grad_full[1], next_dec[0]),
            back_dot(grad_full[1], same_dec[1]),
        ]
    )
    cross_grad = jnp.einsum(
        "td,kcd->ktc", grad_full[2], cross_dec[0], preferred_element_type=jnp.float32
    )
    cross_grad = cross_grad + jnp.einsum(
        "td,kcd->ktc", grad_full[3], far_weight[0], preferred_element_type=jnp.float32
    )
    act_grad = act_grad + cross_grad
    gate_slope = gate_value + pre_act * gate_value * (1.0 - gate_value) / jump_width
    pre_grad = act_grad * gate_slope
    grad_bias = jnp.sum(pre_grad, axis=1)
    pre_rounded = pre_grad.astype(jnp.bfloat16)
    grad_enc = jnp.einsum(
        "ktd,ktc->kdc", inputs_full, pre_rounded, preferred_element_type=jnp.float32
    ).astype(jnp.bfloat16)
    grad_same = jnp.stack(
        [outer_dot(latent_act[0], grad_full[0]), outer_dot(latent_act[1], grad_full[1])]
    ).astype(jnp.bfloat16)
    grad_next = outer_dot(latent_act[0], grad_full[1])[None].astype(jnp.bfloat16)
    near_grad = jnp.einsum(
        "ktc,td->kcd", source_act, grad_full[2], preferred_element_type=jnp.float32
    ).astype(jnp.bfloat16)
    far_grad = jnp.einsum(
        "ktc,td->kcd", source_act, grad_full[3], preferred_element_type=jnp.float32
    ).astype(jnp.bfloat16)
    far_back = shifted(far_grad, "sec", 1)
    grad_cross = jnp.where(leading, near_grad, far_back)[None]
    return (mean_square, grad_enc, grad_bias, grad_same, grad_next, grad_cross)


def solution(mesh):
    in_specs = (
        P("sec", None, "lat"),
        P("sec", None, "lat"),
        P("sec", None, "lat"),
        P("sec", "lat"),
        P("sec", "lat"),
        P("sec", "lat", None),
        P("sec", "lat", None),
        P("sec", None, "lat", None),
    )
    out_specs = (
        P(),
        P("sec", None, "lat"),
        P("sec", "lat"),
        P("sec", "lat", None),
        P("sec", "lat", None),
        P("sec", None, "lat", None),
    )
    return jax.shard_map(
        per_device, mesh=mesh, in_specs=in_specs, out_specs=out_specs, check_vma=False
    )
```

profile of v0, /device:TPU:0, one launch (start us, length us, event | category | flops | bytes accessed | tf_op | source)
XLA Modules:
  0.0 208.9 jit_solution(15887882356919361757)
XLA Ops:
  7.2 0.7 all-gather.3.cloned.1.call-update
  8.0 1.3 collective-permute-start
  9.3 0.7 convert_multiply_fusion
  10.0 39.8 %all-gather.3.cloned.1.call-done = bf16[2,128,2048]{2,1,0:T(8,128)(2,1)} async-done(((bf16[2,128,128]{2,1,0:T(8,128)(2,1)}), bf16[2,128,2048]{2,1,0:T(8,128)(2,1)}) %all-gather.3.cloned.1.call-update) | async-done | bytes 1048592 | tf_op jit(solution)/shard_map/all_gather | solution.py:29
  49.7 1.7 fusion.30
  51.5 1.3 fusion.20
  52.8 0.3 convolution_bitcast_fusion.2
  53.1 0.3 fusion
  53.4 0.4 copy-done.2
  53.8 0.3 convolution_bitcast_fusion.1
  54.1 0.3 convolution_bitcast_fusion
  54.5 2.2 %pad_maximum_fusion = f32[4,128,2048]{2,1,0:T(8,128)} fusion(f32[1,128,2048]{2,1,0:T(8,128)S(1)} %convolution_bitcast_fusion, f32[1,128,2048]{2,1,0:T(8,128)S(1)} %convolution_bitcast_fusion.1, f32[1,128,2048]{2,1,0:T(8,128)S(1)} %fusion, f32[1,128,2048]{2,1,0:T(8,128)S(1)} %convolution_bitcast_fusion.2), kind=kLoop, calls=%fused_computation | loop fusion | flops 3145728 | bytes 8388608 | tf_op jit(solution)/shard_map/stack | solution.py:49
  56.8 71.9 %reduce-scatter.2.cloned.1.call-done = f32[4,128,128]{2,1,0:T(8,128)} async-done(((f32[4,128,2048]{2,1,0:T(8,128)}), f32[4,128,128]{2,1,0:T(8,128)}) %reduce-scatter.2.cloned.1.call-update) | async-done | bytes 262160 | tf_op jit(solution)/shard_map/reduce_scatter | solution.py:50
  128.7 0.9 slice.55
  129.6 3.4 %collective-permute-start.1 = (f32[2,128,128]{2,1,0:T(8,128)S(1)}, f32[2,128,128]{2,1,0:T(8,128)S(1)}, u32[]{:S(2)}, u32[]{:S(2)}) collective-permute-start(f32[2,128,128]{2,1,0:T(8,128)S(1)} %slice.55), channel_id=1, source_target_pairs={{0,16},{1,17},{2,18},{3,19},{4,20},{5,21},{6,22},{7,23},{8,24},{9,... | collective-permute-start | bytes 393224 | tf_op jit(solution)/shard_map/ppermute | solution.py:14
  133.0 2.5 %collective-permute-done.1 = f32[2,128,128]{2,1,0:T(8,128)S(1)} collective-permute-done((f32[2,128,128]{2,1,0:T(8,128)S(1)}, f32[2,128,128]{2,1,0:T(8,128)S(1)}, u32[]{:S(2)}, u32[]{:S(2)}) %collective-permute-start.1) | collective-permute-done | bytes 131104 | tf_op jit(solution)/shard_map/ppermute | solution.py:14
  135.5 1.6 fusion.36
  137.1 1.3 collective-permute-start.2
  138.4 4.9 %collective-permute-done.2 = bf16[2,128,128]{2,1,0:T(8,128)(2,1)S(1)} collective-permute-done((bf16[2,128,128]{2,1,0:T(8,128)(2,1)S(1)}, bf16[2,128,128]{2,1,0:T(8,128)(2,1)S(1)}, u32[]{:S(2)}, u32[]{:S(2)}) %collective-permute-start.2) | collective-permute-done | bytes 65568 | tf_op jit(solution)/shard_map/ppermute | solution.py:14
  143.2 0.7 pad_maximum_fusion.2
  143.9 39.2 %psum.7 = f32[]{:T(128)} all-reduce(f32[]{:T(128)} %get-tuple-element.7), channel_id=1, replica_groups=mesh['sec'=2,'lat'=16] {'sec','lat'}, use_global_device_ids=true, to_apply=%region_2.3 | all-reduce | flops 1 | bytes 8 | tf_op jit(solution)/shard_map/psum | solution.py:54
  183.7 0.5 all-gather.5.cloned.1.call-done
  184.3 1.5 convolution_convert_fusion
  185.7 3.7 %collective-permute-start.3 = (bf16[2,64,2048]{2,1,0:T(8,128)(2,1)S(1)}, bf16[2,64,2048]{2,1,0:T(8,128)(2,1)S(1)}, u32[]{:S(2)}, u32[]{:S(2)}) collective-permute-start(bf16[2,64,2048]{2,1,0:T(8,128)(2,1)S(1)} %convolution_convert_fusion), channel_id=1, source_target_pairs={{0,16},{1,17},{2,18},{3,19},{4,20},{5,21},{6,22},{7,23},{8,24},{9,... | collective-permute-start | bytes 1572872 | tf_op jit(solution)/shard_map/ppermute | solution.py:14
  189.5 1.3 fusion.5
  190.8 1.3 fusion.4
  192.0 0.8 pad_maximum_fusion.1
  194.1 0.9 fusion.6
  195.0 1.0 fusion.41
  196.0 1.1 fusion.3
  197.1 3.0 %collective-permute-done.3 = bf16[2,64,2048]{2,1,0:T(8,128)(2,1)S(1)} collective-permute-done((bf16[2,64,2048]{2,1,0:T(8,128)(2,1)S(1)}, bf16[2,64,2048]{2,1,0:T(8,128)(2,1)S(1)}, u32[]{:S(2)}, u32[]{:S(2)}) %collective-permute-start.3) | collective-permute-done | bytes 524320 | tf_op jit(solution)/shard_map/ppermute | solution.py:14
  200.1 1.1 fusion.2
  (23 shorter events, 1.4 us)
Async XLA Ops:
  7.2 42.6 %copy-start = (bf16[2,2048,64]{1,2,0:T(8,128)(2,1)S(1)}, bf16[2,2048,64]{1,2,0:T(8,128)(2,1)}, u32[]{:S(2)}) copy-start(bf16[2,2048,64]{1,2,0:T(8,128)(2,1)} %param.10) | copy-start | bytes 1572868
  7.2 45.6 %copy-start.4 = (bf16[2,64,2048]{2,1,0:T(8,128)(2,1)S(1)}, bf16[2,64,2048]{2,1,0:T(8,128)(2,1)}, u32[]{:S(2)}) copy-start(bf16[2,64,2048]{2,1,0:T(8,128)(2,1)} %param.13) | copy-start | bytes 1572868
  7.2 42.5 %all-gather.3.cloned.1.call-start = ((), (), s32[]{:S(2)}) async-start(), calls=%async_computation.1 | async-start | bytes 1114112 | tf_op jit(solution)/shard_map/all_gather | solution.py:29
  7.9 120.8 %reduce-scatter.2.cloned.1.call-start = ((), (), s32[]{:S(2)}) async-start(), calls=%async_computation.2 | async-start | bytes 4456448 | tf_op jit(solution)/shard_map/reduce_scatter | solution.py:50
  8.0 46.1 %collective-permute-start = (bf16[1,2,64,2048]{3,2,1,0:T(8,128)(2,1)}, bf16[1,2,64,2048]{3,2,1,0:T(8,128)(2,1)S(1)}, u32[]{:S(2)}, u32[]{:S(2)}) collective-permute-start(bf16[1,2,64,2048]{3,2,1,0:T(8,128)(2,1)} %param.15), channel_id=1, source_target_pairs={{16,0},{17,1},{18,2},{19,3},{20,4},{21,5},{22,6},{23,7},{24,8},{25... | collective-permute-start | bytes 1572872 | tf_op jit(solution)/shard_map/ppermute | solution.py:14
  10.0 43.1 %copy-start.5 = (bf16[1,64,2048]{2,1,0:T(8,128)(2,1)S(1)}, bf16[1,64,2048]{2,1,0:T(8,128)(2,1)}, u32[]{:S(2)}) copy-start(bf16[1,64,2048]{2,1,0:T(8,128)(2,1)} %param.14) | copy-start | bytes 786436
  52.7 1.0 copy-start.2
  56.7 78.8 %copy-start.6 = (bf16[2,128,128]{2,1,0:T(8,128)(2,1)S(1)}, bf16[2,128,128]{2,1,0:T(8,128)(2,1)}, u32[]{:S(2)}) copy-start(bf16[2,128,128]{2,1,0:T(8,128)(2,1)} %param.9) | copy-start | bytes 196612
  56.7 127.5 %all-gather.5.cloned.1.call-start = ((), (), s32[]{:S(2)}) async-start(), calls=%async_computation.3 | async-start | bytes 2228224 | tf_op jit(solution)/shard_map/all_gather | solution.py:58
  129.6 5.9 %collective-permute-start.1 = (f32[2,128,128]{2,1,0:T(8,128)S(1)}, f32[2,128,128]{2,1,0:T(8,128)S(1)}, u32[]{:S(2)}, u32[]{:S(2)}) collective-permute-start(f32[2,128,128]{2,1,0:T(8,128)S(1)} %slice.55), channel_id=1, source_target_pairs={{0,16},{1,17},{2,18},{3,19},{4,20},{5,21},{6,22},{7,23},{8,24},{9,... | collective-permute-start | bytes 393224 | tf_op jit(solution)/shard_map/ppermute | solution.py:14
  137.1 6.1 %collective-permute-start.2 = (bf16[2,128,128]{2,1,0:T(8,128)(2,1)S(1)}, bf16[2,128,128]{2,1,0:T(8,128)(2,1)S(1)}, u32[]{:S(2)}, u32[]{:S(2)}) collective-permute-start(bf16[2,128,128]{2,1,0:T(8,128)(2,1)S(1)} %get-tuple-element.6), channel_id=1, source_target_pairs={{16,0},{17,1},{18,2},{19,3},{20,4},{21,5},{22,6},{23,7},{24,8},{25... | collective-permute-start | bytes 196616 | tf_op jit(solution)/shard_map/ppermute | solution.py:14
  184.3 8.6 %copy-start.1 = (bf16[4,128,2048]{2,1,0:T(8,128)(2,1)S(1)}, bf16[4,128,2048]{2,1,0:T(8,128)(2,1)}, u32[]{:S(2)}) copy-start(bf16[4,128,2048]{2,1,0:T(8,128)(2,1)} %all-gather.5.cloned.1.call-done) | copy-start | bytes 6291460
  185.7 14.4 %collective-permute-start.3 = (bf16[2,64,2048]{2,1,0:T(8,128)(2,1)S(1)}, bf16[2,64,2048]{2,1,0:T(8,128)(2,1)S(1)}, u32[]{:S(2)}, u32[]{:S(2)}) collective-permute-start(bf16[2,64,2048]{2,1,0:T(8,128)(2,1)S(1)} %convolution_convert_fusion), channel_id=1, source_target_pairs={{0,16},{1,17},{2,18},{3,19},{4,20},{5,21},{6,22},{7,23},{8,24},{9,... | collective-permute-start | bytes 1572872 | tf_op jit(solution)/shard_map/ppermute | solution.py:14
  193.5 2.5 %copy-start.3 = (bf16[2,128,2048]{2,1,0:T(8,128)(2,1)S(1)}, bf16[2,128,2048]{2,1,0:T(8,128)(2,1)}, u32[]{:S(2)}) copy-start(bf16[2,128,2048]{2,1,0:T(8,128)(2,1)} %all-gather.3.cloned.1.call-done) | copy-start | bytes 3145732
Sparse Core Ops, SparseCore 0:
  10.2 39.4 all-gather.2
  56.8 71.8 reduce-scatter.1
  144.0 40.1 all-gather.4
where the time goes:
time: 209 us
  waiting for transfers between devices  123 us (59%)
  blocking collectives  39.2 us (19%)
  between operations  15.7 us (8%)
  matrix products  13.5 us (6%)
  starting transfers between devices  9.81 us (5%)
  other arithmetic  5.98 us (3%)
    reduce_scatter x1, waiting for transfers between devices, per_device(): summed = lax.psum_scatter(partials, 'lat', scatter_dimension=2, tiled=True)  71.9 us
    all_gather x1, waiting for transfers between devices, per_device(): inputs_full = lax.all_gather(resid_in, 'lat', axis=2, tiled=True)  39.8 us
    psum x1, blocking collectives, per_device(): squared_total = lax.psum(jnp.sum(misfit * misfit), ('sec', 'lat'))  39.2 us
    ppermute x4, waiting for transfers between devices, shifted(): lax.ppermute(value, axis, [(source, source + steps) for source in range(f...  10.4 us
    ppermute x4, starting transfers between devices, shifted(): lax.ppermute(value, axis, [(source, source + steps) for source in range(f...  9.69 us
  transfers between devices with their start and end apart: 7, of which 6 were waited for; matrix products, arithmetic and copies ran while one was open for 6% of the time, Pallas kernels for 0%

commit v1 on v0

--- a/solution.py
+++ b/solution.py
@@ -2,6 +2,7 @@
 import jax.numpy as jnp
 from jax import lax
 from jax.sharding import PartitionSpec as P
+from jax.lax import axis_index, axis_size, ppermute
 
 D = 2048
 TOKENS = 128
@@ -26,7 +27,18 @@
 
 def per_device(resid_in, mlp_out, enc_weight, enc_bias, thresholds, same_dec, next_dec, cross_dec):
     leading = lax.axis_index("sec") == 0
-    inputs_full = lax.all_gather(resid_in, "lat", axis=2, tiled=True)
+    ledger = [resid_in]
+    it = 0
+    axis_len = axis_size("lat")
+    while it < axis_len - 1:
+        m_next = ppermute(
+            ledger[-1], "lat", [(num, (num + 1) % axis_len) for num in range(axis_len)]
+        )
+        ledger.append(m_next)
+        it += 1
+    work_now = jnp.concatenate(ledger[::-1], axis=2)
+    e_next = axis_index("lat")
+    inputs_full = jnp.roll(work_now, (e_next + 1) * resid_in.shape[2], axis=2)
     pre_act = (
         jnp.einsum("ktd,kdc->ktc", inputs_full, enc_weight, preferred_element_type=jnp.float32)
         + enc_bias[:, None, :]

time: 209 us -> 268 us (1.28)
  waiting for transfers between devices: 123 us -> 175 us
  local copies, waits for them, and re-layouts: 1.32 us -> 6.22 us
    ppermute x0 -> x15, waiting for transfers between devices: none -> 95 us  [per_device(): ppermute(ledger[-1], 'lat', [(num, (num + 1) % axis_len) for num in range...]
    all_gather x1 -> x0, waiting for transfers between devices: 39.8 us -> none  [per_device(): inputs_full = lax.all_gather(resid_in, 'lat', axis=2, tiled=True)]
    unnamed x14 -> x51, local copies, waits for them, and re-layouts: 0.41 us -> 5.28 us
  transfers between devices with their start and end apart: 7 -> 21, of which waited for: 6 -> 20; matrix products, arithmetic and copies ran while one was open for 6% -> 6% of each run, Pallas kernels for 0% -> 0%
where the time goes in v1:
time: 268 us; the launch traced here: 267 us
  waiting for transfers between devices  175 us (65%)
  blocking collectives  39.2 us (15%)
  between operations  16.2 us (6%)
  matrix products  14.1 us (5%)
  starting transfers between devices  10.2 us (4%)
  local copies, waits for them, and re-layouts  6.22 us (2%)
  other arithmetic  5.96 us (2%)
    ppermute x15, waiting for transfers between devices, per_device(): ppermute(ledger[-1], 'lat', [(num, (num + 1) % axis_len) for num in range...  95 us
    reduce_scatter x1, waiting for transfers between devices, per_device(): summed = lax.psum_scatter(partials, 'lat', scatter_dimension=2, tiled=True)  70.5 us
    psum x1, blocking collectives, per_device(): squared_total = lax.psum(jnp.sum(misfit * misfit), ('sec', 'lat'))  39.2 us
    ppermute x4, starting transfers between devices, shifted(): lax.ppermute(value, axis, [(source, source + steps) for source in range(f...  9.58 us
    ppermute x4, waiting for transfers between devices, shifted(): lax.ppermute(value, axis, [(source, source + steps) for source in range(f...  9.33 us
  transfers between devices with their start and end apart: 21, of which 20 were waited for; matrix products, arithmetic and copies ran while one was open for 6% of the time, Pallas kernels for 0%

profile of v1, /device:TPU:0, one launch (start us, length us, event | category | flops | bytes accessed | tf_op | source)
XLA Modules:
  0.0 267.2 jit_solution(1229855023415377547)
XLA Ops:
  7.7 7.2 %collective-permute-done = bf16[2,128,128]{2,1,0:T(8,128)(2,1)S(1)} collective-permute-done((bf16[2,128,128]{2,1,0:T(8,128)(2,1)}, bf16[2,128,128]{2,1,0:T(8,128)(2,1)S(1)}, u32[]{:S(2)}, u32[]{:S(2)}) %collective-permute-start) | collective-permute-done | bytes 65568 | tf_op jit(solution)/shard_map/ppermute | solution.py:34
  14.9 6.4 %collective-permute-done.1 = bf16[2,128,128]{2,1,0:T(8,128)(2,1)S(1)} collective-permute-done((bf16[2,128,128]{2,1,0:T(8,128)(2,1)S(1)}, bf16[2,128,128]{2,1,0:T(8,128)(2,1)S(1)}, u32[]{:S(2)}, u32[]{:S(2)}) %collective-permute-start.1) | collective-permute-done | bytes 65568 | tf_op jit(solution)/shard_map/ppermute | solution.py:34
  21.3 6.4 %collective-permute-done.2 = bf16[2,128,128]{2,1,0:T(8,128)(2,1)S(1)} collective-permute-done((bf16[2,128,128]{2,1,0:T(8,128)(2,1)S(1)}, bf16[2,128,128]{2,1,0:T(8,128)(2,1)S(1)}, u32[]{:S(2)}, u32[]{:S(2)}) %collective-permute-start.2) | collective-permute-done | bytes 65568 | tf_op jit(solution)/shard_map/ppermute | solution.py:34
  27.7 6.4 %collective-permute-done.3 = bf16[2,128,128]{2,1,0:T(8,128)(2,1)S(1)} collective-permute-done((bf16[2,128,128]{2,1,0:T(8,128)(2,1)S(1)}, bf16[2,128,128]{2,1,0:T(8,128)(2,1)S(1)}, u32[]{:S(2)}, u32[]{:S(2)}) %collective-permute-start.3) | collective-permute-done | bytes 65568 | tf_op jit(solution)/shard_map/ppermute | solution.py:34
  34.1 6.4 %collective-permute-done.4 = bf16[2,128,128]{2,1,0:T(8,128)(2,1)S(1)} collective-permute-done((bf16[2,128,128]{2,1,0:T(8,128)(2,1)S(1)}, bf16[2,128,128]{2,1,0:T(8,128)(2,1)S(1)}, u32[]{:S(2)}, u32[]{:S(2)}) %collective-permute-start.4) | collective-permute-done | bytes 65568 | tf_op jit(solution)/shard_map/ppermute | solution.py:34
  40.5 6.4 %collective-permute-done.5 = bf16[2,128,128]{2,1,0:T(8,128)(2,1)S(1)} collective-permute-done((bf16[2,128,128]{2,1,0:T(8,128)(2,1)S(1)}, bf16[2,128,128]{2,1,0:T(8,128)(2,1)S(1)}, u32[]{:S(2)}, u32[]{:S(2)}) %collective-permute-start.5) | collective-permute-done | bytes 65568 | tf_op jit(solution)/shard_map/ppermute | solution.py:34
  46.8 6.4 %collective-permute-done.6 = bf16[2,128,128]{2,1,0:T(8,128)(2,1)S(1)} collective-permute-done((bf16[2,128,128]{2,1,0:T(8,128)(2,1)S(1)}, bf16[2,128,128]{2,1,0:T(8,128)(2,1)S(1)}, u32[]{:S(2)}, u32[]{:S(2)}) %collective-permute-start.6) | collective-permute-done | bytes 65568 | tf_op jit(solution)/shard_map/ppermute | solution.py:34
  53.2 6.4 %collective-permute-done.7 = bf16[2,128,128]{2,1,0:T(8,128)(2,1)S(1)} collective-permute-done((bf16[2,128,128]{2,1,0:T(8,128)(2,1)S(1)}, bf16[2,128,128]{2,1,0:T(8,128)(2,1)S(1)}, u32[]{:S(2)}, u32[]{:S(2)}) %collective-permute-start.7) | collective-permute-done | bytes 65568 | tf_op jit(solution)/shard_map/ppermute | solution.py:34
  59.6 6.4 %collective-permute-done.8 = bf16[2,128,128]{2,1,0:T(8,128)(2,1)S(1)} collective-permute-done((bf16[2,128,128]{2,1,0:T(8,128)(2,1)S(1)}, bf16[2,128,128]{2,1,0:T(8,128)(2,1)S(1)}, u32[]{:S(2)}, u32[]{:S(2)}) %collective-permute-start.8) | collective-permute-done | bytes 65568 | tf_op jit(solution)/shard_map/ppermute | solution.py:34
  66.0 6.4 %collective-permute-done.9 = bf16[2,128,128]{2,1,0:T(8,128)(2,1)S(1)} collective-permute-done((bf16[2,128,128]{2,1,0:T(8,128)(2,1)S(1)}, bf16[2,128,128]{2,1,0:T(8,128)(2,1)S(1)}, u32[]{:S(2)}, u32[]{:S(2)}) %collective-permute-start.9) | collective-permute-done | bytes 65568 | tf_op jit(solution)/shard_map/ppermute | solution.py:34
  72.4 6.4 %collective-permute-done.10 = bf16[2,128,128]{2,1,0:T(8,128)(2,1)S(1)} collective-permute-done((bf16[2,128,128]{2,1,0:T(8,128)(2,1)S(1)}, bf16[2,128,128]{2,1,0:T(8,128)(2,1)S(1)}, u32[]{:S(2)}, u32[]{:S(2)}) %collective-permute-start.10) | collective-permute-done | bytes 65568 | tf_op jit(solution)/shard_map/ppermute | solution.py:34
  78.8 6.4 %collective-permute-done.11 = bf16[2,128,128]{2,1,0:T(8,128)(2,1)S(1)} collective-permute-done((bf16[2,128,128]{2,1,0:T(8,128)(2,1)S(1)}, bf16[2,128,128]{2,1,0:T(8,128)(2,1)S(1)}, u32[]{:S(2)}, u32[]{:S(2)}) %collective-permute-start.11) | collective-permute-done | bytes 65568 | tf_op jit(solution)/shard_map/ppermute | solution.py:34
  85.2 6.4 %collective-permute-done.12 = bf16[2,128,128]{2,1,0:T(8,128)(2,1)S(1)} collective-permute-done((bf16[2,128,128]{2,1,0:T(8,128)(2,1)S(1)}, bf16[2,128,128]{2,1,0:T(8,128)(2,1)S(1)}, u32[]{:S(2)}, u32[]{:S(2)}) %collective-permute-start.12) | collective-permute-done | bytes 65568 | tf_op jit(solution)/shard_map/ppermute | solution.py:34
  91.6 1.3 collective-permute-start.15
  92.9 5.2 %collective-permute-done.13 = bf16[2,128,128]{2,1,0:T(8,128)(2,1)} collective-permute-done((bf16[2,128,128]{2,1,0:T(8,128)(2,1)S(1)}, bf16[2,128,128]{2,1,0:T(8,128)(2,1)}, u32[]{:S(2)}, u32[]{:S(2)}) %collective-permute-start.13) | collective-permute-done | bytes 65568 | tf_op jit(solution)/shard_map/ppermute | solution.py:34
  98.7 6.0 %collective-permute-done.14 = bf16[2,128,128]{2,1,0:T(8,128)(2,1)} collective-permute-done((bf16[2,128,128]{2,1,0:T(8,128)(2,1)}, bf16[2,128,128]{2,1,0:T(8,128)(2,1)}, u32[]{:S(2)}, u32[]{:S(2)}) %collective-permute-start.14) | collective-permute-done | bytes 65568 | tf_op jit(solution)/shard_map/ppermute | solution.py:34
  109.9 1.1 fusion.31
  112.7 1.4 convolution_bitcast_fusion
  114.1 2.2 pad_maximum_fusion
  116.3 70.5 %reduce-scatter.2.cloned.1.call-done = f32[4,128,128]{2,1,0:T(8,128)} async-done(((f32[4,128,2048]{2,1,0:T(8,128)}), f32[4,128,128]{2,1,0:T(8,128)}) %reduce-scatter.2.cloned.1.call-update) | async-done | bytes 262160 | tf_op jit(solution)/shard_map/reduce_scatter | solution.py:62
  187.8 3.3 %collective-permute-start.16 = (f32[2,128,128]{2,1,0:T(8,128)S(1)}, f32[2,128,128]{2,1,0:T(8,128)S(1)}, u32[]{:S(2)}, u32[]{:S(2)}) collective-permute-start(f32[2,128,128]{2,1,0:T(8,128)S(1)} %slice.55), channel_id=1, source_target_pairs={{0,16},{1,17},{2,18},{3,19},{4,20},{5,21},{6,22},{7,23},{8,24},{9,... | collective-permute-start | bytes 393224 | tf_op jit(solution)/shard_map/ppermute | solution.py:15
  191.1 2.5 collective-permute-done.16
  193.6 1.6 fusion.37
  195.1 1.3 collective-permute-start.17
  196.4 4.9 %collective-permute-done.17 = bf16[2,128,128]{2,1,0:T(8,128)(2,1)S(1)} collective-permute-done((bf16[2,128,128]{2,1,0:T(8,128)(2,1)S(1)}, bf16[2,128,128]{2,1,0:T(8,128)(2,1)S(1)}, u32[]{:S(2)}, u32[]{:S(2)}) %collective-permute-start.17) | collective-permute-done | bytes 65568 | tf_op jit(solution)/shard_map/ppermute | solution.py:15
  201.9 39.2 %psum.7 = f32[]{:T(128)} all-reduce(f32[]{:T(128)} %get-tuple-element.7), channel_id=1, replica_groups=mesh['sec'=2,'lat'=16] {'sec','lat'}, use_global_device_ids=true, to_apply=%region_2.3 | all-reduce | flops 1 | bytes 8 | tf_op jit(solution)/shard_map/psum | solution.py:66
  242.3 1.5 convolution_convert_fusion.1
  243.8 3.7 %collective-permute-start.18 = (bf16[2,64,2048]{2,1,0:T(8,128)(2,1)S(1)}, bf16[2,64,2048]{2,1,0:T(8,128)(2,1)S(1)}, u32[]{:S(2)}, u32[]{:S(2)}) collective-permute-start(bf16[2,64,2048]{2,1,0:T(8,128)(2,1)S(1)} %convolution_convert_fusion.1), channel_id=1, source_target_pairs={{0,16},{1,17},{2,18},{3,19},{4,20},{5,21},{6,22},{7,23},{8,24},{9,... | collective-permute-start | bytes 1572872 | tf_op jit(solution)/shard_map/ppermute | solution.py:15
  247.6 1.3 fusion.4
  248.8 1.3 fusion.3
  253.1 2.0 fusion.44
  256.2 2.0 collective-permute-done.18
  (88 shorter events, 15.2 us)
Async XLA Ops:
  7.2 102.7 %copy-start = (bf16[2,2048,64]{1,2,0:T(8,128)(2,1)S(1)}, bf16[2,2048,64]{1,2,0:T(8,128)(2,1)}, u32[]{:S(2)}) copy-start(bf16[2,2048,64]{1,2,0:T(8,128)(2,1)} %param.10) | copy-start | bytes 1572868
  7.2 102.6 %copy-start.6 = (bf16[2,128,128]{2,1,0:T(8,128)(2,1)S(1)}, bf16[2,128,128]{2,1,0:T(8,128)(2,1)}, u32[]{:S(2)}) copy-start(bf16[2,128,128]{2,1,0:T(8,128)(2,1)} %param.8) | copy-start | bytes 196612
  7.2 179.7 %reduce-scatter.2.cloned.1.call-start = ((), (), s32[]{:S(2)}) async-start(), calls=%async_computation.1 | async-start | bytes 4456448 | tf_op jit(solution)/shard_map/reduce_scatter | solution.py:62
  7.2 7.7 %collective-permute-start = (bf16[2,128,128]{2,1,0:T(8,128)(2,1)}, bf16[2,128,128]{2,1,0:T(8,128)(2,1)S(1)}, u32[]{:S(2)}, u32[]{:S(2)}) collective-permute-start(bf16[2,128,128]{2,1,0:T(8,128)(2,1)} %param.8), channel_id=1, source_target_pairs={{0,1},{1,2},{2,3},{3,4},{4,5},{5,6},{6,7},{7,8},{8,9},{9,10},{10,1... | collective-permute-start | bytes 196616 | tf_op jit(solution)/shard_map/ppermute | solution.py:34
  14.9 6.4 %collective-permute-start.1 = (bf16[2,128,128]{2,1,0:T(8,128)(2,1)S(1)}, bf16[2,128,128]{2,1,0:T(8,128)(2,1)S(1)}, u32[]{:S(2)}, u32[]{:S(2)}) collective-permute-start(bf16[2,128,128]{2,1,0:T(8,128)(2,1)S(1)} %collective-permute-done), channel_id=1, source_target_pairs={{0,1},{1,2},{2,3},{3,4},{4,5},{5,6},{6,7},{7,8},{8,9},{9,10},{10,1... | collective-permute-start | bytes 196616 | tf_op jit(solution)/shard_map/ppermute | solution.py:34
  21.3 6.4 %collective-permute-start.2 = (bf16[2,128,128]{2,1,0:T(8,128)(2,1)S(1)}, bf16[2,128,128]{2,1,0:T(8,128)(2,1)S(1)}, u32[]{:S(2)}, u32[]{:S(2)}) collective-permute-start(bf16[2,128,128]{2,1,0:T(8,128)(2,1)S(1)} %collective-permute-done.1), channel_id=1, source_target_pairs={{0,1},{1,2},{2,3},{3,4},{4,5},{5,6},{6,7},{7,8},{8,9},{9,10},{10,1... | collective-permute-start | bytes 196616 | tf_op jit(solution)/shard_map/ppermute | solution.py:34
  27.7 6.4 %collective-permute-start.3 = (bf16[2,128,128]{2,1,0:T(8,128)(2,1)S(1)}, bf16[2,128,128]{2,1,0:T(8,128)(2,1)S(1)}, u32[]{:S(2)}, u32[]{:S(2)}) collective-permute-start(bf16[2,128,128]{2,1,0:T(8,128)(2,1)S(1)} %collective-permute-done.2), channel_id=1, source_target_pairs={{0,1},{1,2},{2,3},{3,4},{4,5},{5,6},{6,7},{7,8},{8,9},{9,10},{10,1... | collective-permute-start | bytes 196616 | tf_op jit(solution)/shard_map/ppermute | solution.py:34
  34.1 6.4 %collective-permute-start.4 = (bf16[2,128,128]{2,1,0:T(8,128)(2,1)S(1)}, bf16[2,128,128]{2,1,0:T(8,128)(2,1)S(1)}, u32[]{:S(2)}, u32[]{:S(2)}) collective-permute-start(bf16[2,128,128]{2,1,0:T(8,128)(2,1)S(1)} %collective-permute-done.3), channel_id=1, source_target_pairs={{0,1},{1,2},{2,3},{3,4},{4,5},{5,6},{6,7},{7,8},{8,9},{9,10},{10,1... | collective-permute-start | bytes 196616 | tf_op jit(solution)/shard_map/ppermute | solution.py:34
  40.5 6.4 %collective-permute-start.5 = (bf16[2,128,128]{2,1,0:T(8,128)(2,1)S(1)}, bf16[2,128,128]{2,1,0:T(8,128)(2,1)S(1)}, u32[]{:S(2)}, u32[]{:S(2)}) collective-permute-start(bf16[2,128,128]{2,1,0:T(8,128)(2,1)S(1)} %collective-permute-done.4), channel_id=1, source_target_pairs={{0,1},{1,2},{2,3},{3,4},{4,5},{5,6},{6,7},{7,8},{8,9},{9,10},{10,1... | collective-permute-start | bytes 196616 | tf_op jit(solution)/shard_map/ppermute | solution.py:34
  46.8 6.4 %collective-permute-start.6 = (bf16[2,128,128]{2,1,0:T(8,128)(2,1)S(1)}, bf16[2,128,128]{2,1,0:T(8,128)(2,1)S(1)}, u32[]{:S(2)}, u32[]{:S(2)}) collective-permute-start(bf16[2,128,128]{2,1,0:T(8,128)(2,1)S(1)} %collective-permute-done.5), channel_id=1, source_target_pairs={{0,1},{1,2},{2,3},{3,4},{4,5},{5,6},{6,7},{7,8},{8,9},{9,10},{10,1... | collective-permute-start | bytes 196616 | tf_op jit(solution)/shard_map/ppermute | solution.py:34
  53.2 6.4 %collective-permute-start.7 = (bf16[2,128,128]{2,1,0:T(8,128)(2,1)S(1)}, bf16[2,128,128]{2,1,0:T(8,128)(2,1)S(1)}, u32[]{:S(2)}, u32[]{:S(2)}) collective-permute-start(bf16[2,128,128]{2,1,0:T(8,128)(2,1)S(1)} %collective-permute-done.6), channel_id=1, source_target_pairs={{0,1},{1,2},{2,3},{3,4},{4,5},{5,6},{6,7},{7,8},{8,9},{9,10},{10,1... | collective-permute-start | bytes 196616 | tf_op jit(solution)/shard_map/ppermute | solution.py:34
  59.6 6.4 %collective-permute-start.8 = (bf16[2,128,128]{2,1,0:T(8,128)(2,1)S(1)}, bf16[2,128,128]{2,1,0:T(8,128)(2,1)S(1)}, u32[]{:S(2)}, u32[]{:S(2)}) collective-permute-start(bf16[2,128,128]{2,1,0:T(8,128)(2,1)S(1)} %collective-permute-done.7), channel_id=1, source_target_pairs={{0,1},{1,2},{2,3},{3,4},{4,5},{5,6},{6,7},{7,8},{8,9},{9,10},{10,1... | collective-permute-start | bytes 196616 | tf_op jit(solution)/shard_map/ppermute | solution.py:34
  66.0 6.4 %collective-permute-start.9 = (bf16[2,128,128]{2,1,0:T(8,128)(2,1)S(1)}, bf16[2,128,128]{2,1,0:T(8,128)(2,1)S(1)}, u32[]{:S(2)}, u32[]{:S(2)}) collective-permute-start(bf16[2,128,128]{2,1,0:T(8,128)(2,1)S(1)} %collective-permute-done.8), channel_id=1, source_target_pairs={{0,1},{1,2},{2,3},{3,4},{4,5},{5,6},{6,7},{7,8},{8,9},{9,10},{10,1... | collective-permute-start | bytes 196616 | tf_op jit(solution)/shard_map/ppermute | solution.py:34
  72.4 6.4 %collective-permute-start.10 = (bf16[2,128,128]{2,1,0:T(8,128)(2,1)S(1)}, bf16[2,128,128]{2,1,0:T(8,128)(2,1)S(1)}, u32[]{:S(2)}, u32[]{:S(2)}) collective-permute-start(bf16[2,128,128]{2,1,0:T(8,128)(2,1)S(1)} %collective-permute-done.9), channel_id=1, source_target_pairs={{0,1},{1,2},{2,3},{3,4},{4,5},{5,6},{6,7},{7,8},{8,9},{9,10},{10,1... | collective-permute-start | bytes 196616 | tf_op jit(solution)/shard_map/ppermute | solution.py:34
  78.8 6.4 %collective-permute-start.11 = (bf16[2,128,128]{2,1,0:T(8,128)(2,1)S(1)}, bf16[2,128,128]{2,1,0:T(8,128)(2,1)S(1)}, u32[]{:S(2)}, u32[]{:S(2)}) collective-permute-start(bf16[2,128,128]{2,1,0:T(8,128)(2,1)S(1)} %collective-permute-done.10), channel_id=1, source_target_pairs={{0,1},{1,2},{2,3},{3,4},{4,5},{5,6},{6,7},{7,8},{8,9},{9,10},{10,1... | collective-permute-start | bytes 196616 | tf_op jit(solution)/shard_map/ppermute | solution.py:34
  85.2 6.4 %collective-permute-start.12 = (bf16[2,128,128]{2,1,0:T(8,128)(2,1)S(1)}, bf16[2,128,128]{2,1,0:T(8,128)(2,1)S(1)}, u32[]{:S(2)}, u32[]{:S(2)}) collective-permute-start(bf16[2,128,128]{2,1,0:T(8,128)(2,1)S(1)} %collective-permute-done.11), channel_id=1, source_target_pairs={{0,1},{1,2},{2,3},{3,4},{4,5},{5,6},{6,7},{7,8},{8,9},{9,10},{10,1... | collective-permute-start | bytes 196616 | tf_op jit(solution)/shard_map/ppermute | solution.py:34
  91.6 6.5 %collective-permute-start.13 = (bf16[2,128,128]{2,1,0:T(8,128)(2,1)S(1)}, bf16[2,128,128]{2,1,0:T(8,128)(2,1)}, u32[]{:S(2)}, u32[]{:S(2)}) collective-permute-start(bf16[2,128,128]{2,1,0:T(8,128)(2,1)S(1)} %collective-permute-done.12), channel_id=1, source_target_pairs={{0,1},{1,2},{2,3},{3,4},{4,5},{5,6},{6,7},{7,8},{8,9},{9,10},{10,1... | collective-permute-start | bytes 196616 | tf_op jit(solution)/shard_map/ppermute | solution.py:34
  91.6 21.1 %collective-permute-start.15 = (bf16[1,2,64,2048]{3,2,1,0:T(8,128)(2,1)}, bf16[1,2,64,2048]{3,2,1,0:T(8,128)(2,1)}, u32[]{:S(2)}, u32[]{:S(2)}) collective-permute-start(bf16[1,2,64,2048]{3,2,1,0:T(8,128)(2,1)} %param.15), channel_id=1, source_target_pairs={{16,0},{17,1},{18,2},{19,3},{20,4},{21,5},{22,6},{23,7},{24,8},{25... | collective-permute-start | bytes 1572872 | tf_op jit(solution)/shard_map/ppermute | solution.py:15
  98.1 6.7 %collective-permute-start.14 = (bf16[2,128,128]{2,1,0:T(8,128)(2,1)}, bf16[2,128,128]{2,1,0:T(8,128)(2,1)}, u32[]{:S(2)}, u32[]{:S(2)}) collective-permute-start(bf16[2,128,128]{2,1,0:T(8,128)(2,1)} %collective-permute-done.13), channel_id=1, source_target_pairs={{0,1},{1,2},{2,3},{3,4},{4,5},{5,6},{6,7},{7,8},{8,9},{9,10},{10,1... | collective-permute-start | bytes 196616 | tf_op jit(solution)/shard_map/ppermute | solution.py:34
  98.7 11.1 %copy-start.8 = (f32[2,64]{1,0:T(2,128)S(1)}, f32[2,64]{1,0:T(2,128)}, u32[]{:S(2)}) copy-start(f32[2,64]{1,0:T(2,128)} %param.11) | copy-start | bytes 1540
  106.8 4.2 %copy-start.3 = (bf16[2,64,2048]{2,1,0:T(8,128)(2,1)S(1)}, bf16[2,64,2048]{2,1,0:T(8,128)(2,1)}, u32[]{:S(2)}) copy-start(bf16[2,64,2048]{2,1,0:T(8,128)(2,1)} %param.13) | copy-start | bytes 1572868
  109.9 1.8 copy-start.5
  111.3 1.0 copy-start.2
  116.3 77.3 %copy-start.7 = (bf16[2,128,128]{2,1,0:T(8,128)(2,1)S(1)}, bf16[2,128,128]{2,1,0:T(8,128)(2,1)}, u32[]{:S(2)}) copy-start(bf16[2,128,128]{2,1,0:T(8,128)(2,1)} %param.9) | copy-start | bytes 196612
  116.3 126.0 %all-gather.2.cloned.1.call-start = ((), (), s32[]{:S(2)}) async-start(), calls=%async_computation.2 | async-start | bytes 2228224 | tf_op jit(solution)/shard_map/all_gather | solution.py:70
  187.8 5.8 %collective-permute-start.16 = (f32[2,128,128]{2,1,0:T(8,128)S(1)}, f32[2,128,128]{2,1,0:T(8,128)S(1)}, u32[]{:S(2)}, u32[]{:S(2)}) collective-permute-start(f32[2,128,128]{2,1,0:T(8,128)S(1)} %slice.55), channel_id=1, source_target_pairs={{0,16},{1,17},{2,18},{3,19},{4,20},{5,21},{6,22},{7,23},{8,24},{9,... | collective-permute-start | bytes 393224 | tf_op jit(solution)/shard_map/ppermute | solution.py:15
  195.1 6.1 %collective-permute-start.17 = (bf16[2,128,128]{2,1,0:T(8,128)(2,1)S(1)}, bf16[2,128,128]{2,1,0:T(8,128)(2,1)S(1)}, u32[]{:S(2)}, u32[]{:S(2)}) collective-permute-start(bf16[2,128,128]{2,1,0:T(8,128)(2,1)S(1)} %get-tuple-element.6), channel_id=1, source_target_pairs={{16,0},{17,1},{18,2},{19,3},{20,4},{21,5},{22,6},{23,7},{24,8},{25... | collective-permute-start | bytes 196616 | tf_op jit(solution)/shard_map/ppermute | solution.py:15
  242.3 8.6 %copy-start.1 = (bf16[4,128,2048]{2,1,0:T(8,128)(2,1)S(1)}, bf16[4,128,2048]{2,1,0:T(8,128)(2,1)}, u32[]{:S(2)}) copy-start(bf16[4,128,2048]{2,1,0:T(8,128)(2,1)} %all-gather.2.cloned.1.call-done) | copy-start | bytes 6291460
  242.3 8.6 %copy-start.4 = (bf16[2,64,2048]{2,1,0:T(8,128)(2,1)S(1)}, bf16[2,64,2048]{2,1,0:T(8,128)(2,1)}, u32[]{:S(2)}) copy-start(bf16[2,64,2048]{2,1,0:T(8,128)(2,1)} %param.13) | copy-start | bytes 1572868
  243.8 14.4 %collective-permute-start.18 = (bf16[2,64,2048]{2,1,0:T(8,128)(2,1)S(1)}, bf16[2,64,2048]{2,1,0:T(8,128)(2,1)S(1)}, u32[]{:S(2)}, u32[]{:S(2)}) collective-permute-start(bf16[2,64,2048]{2,1,0:T(8,128)(2,1)S(1)} %convolution_convert_fusion.1), channel_id=1, source_target_pairs={{0,16},{1,17},{2,18},{3,19},{4,20},{5,21},{6,22},{7,23},{8,24},{9,... | collective-permute-start | bytes 1572872 | tf_op jit(solution)/shard_map/ppermute | solution.py:15
  251.3 1.9 copy-start.9
Sparse Core Ops, SparseCore 0:
  116.4 70.3 reduce-scatter.1
  202.1 40.2 all-gather.1
